TPU v7x, 512 devices: a whole 4x4x16 slice. The times are simulated.
512 devices in a mesh: query: 32 (over z, core), passage: 16 (over x, y).
Axes of the slice: x: 4, y: 4, z: 16, core: 2. Of those that a mesh axis runs over, the one named last changes fastest.
Arguments:
- queries: bfloat16 [2048, 32, 128], P(('query', 'passage')), may hold values from -60 to 60
- hidden: bfloat16 [2048, 180, 768], P(('query', 'passage')), may hold values from -24 to 24
- proj: bfloat16 [768, 128], replicated, may hold values from -0.21875 to 0.21875
- lists: int32 [2048, 64], P(('query', 'passage')), may hold values from 0 to 63
Outputs:
- losses: float32 [2048], P(('query', 'passage'))
- w_grad: float32 [768, 128], P('passage')
Inputs may be any that keep to these rules, and one draw needn't show every extreme that they name: `lists`: queries of one row only list passages of that same row; entry 0 of each list is the query's positive passage.
All inputs are finite; a program needn't handle non-finite values.
Results may differ from a plain program's by a relative error of at most 0.0075.
The roundings to bfloat16 on the way count: a program that leaves them out, or rounds other values in their place, can miss the bound.
Values may be sent and summed in bfloat16 or wider, within the bound.
A program may use at most 64 MiB of HBM per device.

v0:
```python
import jax
import jax.numpy as jnp
from jax import lax
from jax.sharding import PartitionSpec as P

BETA = 4.0
EPS = 1e-06


def body(queries, hidden, proj, lists):
    qcount, qtok, width = queries.shape
    pcount, ptok, hwidth = hidden.shape
    nside = lax.axis_size("passage")
    prow = pcount * nside
    total = qcount * lax.axis_size("query") * nside
    hidden_flat = hidden.reshape(-1, hwidth)
    flat = jnp.dot(hidden_flat, proj, preferred_element_type=jnp.float32)
    norm = jnp.sqrt(jnp.sum(flat * flat, axis=1, keepdims=True) + EPS)
    unit = flat / norm
    embed = unit.astype(jnp.bfloat16).reshape(pcount, ptok, width)
    gathered = lax.all_gather(queries, "passage", axis=0, tiled=True)
    qflat = gathered.reshape(-1, width)

    def score_single(emb):
        sims = lax.dot_general(
            emb, qflat, (((1,), (1,)), ((), ())), preferred_element_type=jnp.float32
        )
        lse = jax.nn.logsumexp(BETA * sims, axis=0)
        return jnp.sum(lse.reshape(-1, qtok), axis=1) / BETA

    scores = lax.map(score_single, embed).T
    mine = lax.all_to_all(scores, "passage", split_axis=0, concat_axis=1, tiled=True)
    columns = jnp.arange(prow, dtype=jnp.int32)
    onehot = (lists[:, :, None] == columns[None, None, :]).astype(jnp.float32)
    listed = jnp.einsum("qkp,qp->qk", onehot, mine, precision=lax.Precision.HIGHEST)
    losses = jax.nn.logsumexp(listed, axis=1) - listed[:, 0]
    probs = jax.nn.softmax(listed, axis=1)
    target = (jnp.arange(listed.shape[1], dtype=jnp.int32) == 0).astype(jnp.float32)
    coef = (
        jnp.einsum("qkp,qk->qp", onehot, probs - target[None, :], precision=lax.Precision.HIGHEST)
        / total
    )
    coef_home = lax.all_to_all(coef, "passage", split_axis=1, concat_axis=0, tiled=True)
    grad_qflat = gathered.reshape(-1, width)

    def grad_single(args):
        emb, column = args
        sims = lax.dot_general(
            emb, grad_qflat, (((1,), (1,)), ((), ())), preferred_element_type=jnp.float32
        )
        probs = jax.nn.softmax(BETA * sims, axis=0)
        weight = (probs * jnp.repeat(column, qtok)[None, :]).astype(jnp.bfloat16)
        return jnp.dot(weight, grad_qflat, preferred_element_type=jnp.float32)

    d_embed = lax.map(grad_single, (embed, coef_home.T))
    d_rows = d_embed.reshape(-1, width)
    d_flat = ((d_rows - unit * jnp.sum(d_rows * unit, axis=1, keepdims=True)) / norm).astype(
        jnp.bfloat16
    )
    partial_grad = lax.dot_general(
        hidden_flat, d_flat, (((0,), (0,)), ((), ())), preferred_element_type=jnp.float32
    )
    share = hwidth // nside
    full_grad = lax.psum(partial_grad, ("query", "passage"))
    w_grad = lax.dynamic_slice_in_dim(full_grad, lax.axis_index("passage") * share, share, 0)
    return (losses, w_grad)


def solution(mesh):
    placed = (
        P(("query", "passage"), None, None),
        P(("query", "passage"), None, None),
        P(),
        P(("query", "passage"), None),
    )
    return jax.shard_map(
        body,
        mesh=mesh,
        in_specs=placed,
        out_specs=(P(("query", "passage")), P("passage", None)),
        check_vma=False,
    )
```

profile of v0, /device:TPU:2, one launch (start us, length us, event | category | flops | bytes accessed | tf_op | source)
XLA Modules:
  0.0 561.4 jit_solution(6270691283780664740)
XLA Ops:
  7.2 1.4 copy.11
  8.6 0.3 reshape.64
  8.9 0.5 multiply_reduce_fusion.1
  9.5 0.2 fusion.19
  9.6 0.5 copy-done.1
  10.2 26.8 %all_gather.3 = bf16[64,32,128]{2,1,0:T(8,128)(2,1)S(1)} all-gather(bf16[4,32,128]{2,1,0:T(8,128)(2,1)S(1)} %copy-done.6), channel_id=1, replica_groups=mesh['query'=32,'passage'=16] {'passage'}, dimensions={0}, use_global_device_ids=true | all-gather | bytes 557056 | tf_op jit(solution)/shard_map/all_gather | solution.py:21
  37.0 4.4 while.20
  37.1 0.5 fusion.40
  37.6 0.2 exponential_reduce_fusion.3
  38.2 0.5 fusion.40
  38.7 0.2 exponential_reduce_fusion.3
  39.2 0.5 fusion.40
  39.8 0.2 exponential_reduce_fusion.3
  40.3 0.5 fusion.40
  40.9 0.2 exponential_reduce_fusion.3
  41.5 0.6 copy.12
  42.1 5.4 all-to-all-start
  47.6 6.2 %all-to-all-done = f32[16,4,4]{1,2,0:T(4,128)S(1)} async-done(((f32[16,4,4]{1,2,0:T(4,128)}), f32[16,4,4]{1,2,0:T(4,128)S(1)}, u32[]{:S(2)}, u32[]{:S(2)}) %all-to-all-start) | async-done | bytes 1056 | tf_op jit(solution)/shard_map/all_to_all | solution.py:32
  53.9 0.3 fusion.14
  54.3 0.6 fusion.17
  55.1 0.3 fusion.13
  55.5 0.6 copy.14
  56.1 4.8 all-to-all-start.1
  60.9 6.2 %all-to-all-done.1 = f32[4,16,4]{2,0,1:T(4,128)S(1)} async-done(((f32[4,16,4]{2,0,1:T(4,128)}), f32[4,16,4]{2,0,1:T(4,128)S(1)}, u32[]{:S(2)}, u32[]{:S(2)}) %all-to-all-start.1) | async-done | bytes 1056 | tf_op jit(solution)/shard_map/all_to_all | solution.py:43
  67.2 16.0 %while.21 = (s32[]{:T(128)}, f32[4,180,128]{2,1,0:T(8,128)}, bf16[4,180,128]{2,1,0:T(8,128)(2,1)S(1)}, bf16[2048,128]{1,0:T(8,128)(2,1)S(1)}, f32[4,64]{1,0:T(4,128)S(1)}, /*index=5*/s32[]{:T(128)}) while((s32[]{:T(128)}, f32[4,180,128]{2,1,0:T(8,128)}, bf16[4,180,128]{2,1,0:T(8,128)(2,1)S(1)}, bf16[2048,128]{1,0:T(8,128)(2,1)S(1)}, ...), condition=%wide.region_12.13_spmd, body=%wide.region_9.0_spmd.sunk | while | flops 191688704 | bytes 5761993 | solution.py:55
  67.2 1.1 fusion.44
  68.4 0.7 mul.57
  69.1 1.0 fusion.46
  70.1 1.1 fusion.47
  71.2 1.1 fusion.44
  72.4 0.7 mul.57
  73.1 1.0 fusion.46
  74.1 1.1 fusion.47
  75.2 1.1 fusion.44
  76.4 0.7 mul.57
  77.1 1.0 fusion.46
  78.1 1.1 fusion.47
  79.3 1.1 fusion.44
  80.5 0.7 mul.57
  81.1 1.0 fusion.46
  82.2 1.1 fusion.47
  83.3 1.0 reshape.67
  84.3 1.3 multiply_reduce_fusion
  85.6 2.3 convolution_bitcast_fusion.1
  88.0 1.2 fusion.18
  89.2 463.7 %all-reduce.2.cloned.1.call-done = f32[768,128]{0,1:T(8,128)} async-done(((f32[768,128]{0,1:T(8,128)}), f32[768,128]{0,1:T(8,128)}) %all-reduce.2.cloned.1.call-update) | async-done | bytes 393232 | tf_op jit(solution)/shard_map/psum | solution.py:64
  552.8 1.0 constant_dynamic-slice_fusion.1
  553.8 0.7 copy.16
  (102 shorter events, 2.4 us)
Async XLA Ops:
  7.2 1.7 copy-start
  8.9 1.3 copy-start.6
  9.4 0.7 copy-start.1
  9.5 0.7 copy-start.5
  37.0 16.8 %copy-start.12 = (s32[4,64]{1,0:T(4,128)S(1)}, s32[4,64]{1,0:T(4,128)}, u32[]{:S(2)}) copy-start(s32[4,64]{1,0:T(4,128)} %param.11) | copy-start | bytes 3076
  42.1 11.6 %all-to-all-start = ((f32[16,4,4]{1,2,0:T(4,128)}), f32[16,4,4]{1,2,0:T(4,128)S(1)}, u32[]{:S(2)}, u32[]{:S(2)}) async-start(f32[16,4,4]{1,2,0:T(4,128)} %copy.12), calls=%async_computation | async-start | bytes 65536 | tf_op jit(solution)/shard_map/all_to_all | solution.py:32
  54.2 13.0 %copy-start.3 = (f32[4,1,64]{0,2,1:T(8,128)}, f32[4,1,64]{0,2,1:T(8,128)S(1)}, u32[]{:S(2)}) copy-start(f32[4,1,64]{0,2,1:T(8,128)S(1)} %copy.18) | copy-start | bytes 3076
  54.3 0.6 copy-start.7
  56.1 11.1 %all-to-all-start.1 = ((f32[4,16,4]{2,0,1:T(4,128)}), f32[4,16,4]{2,0,1:T(4,128)S(1)}, u32[]{:S(2)}, u32[]{:S(2)}) async-start(f32[4,16,4]{2,0,1:T(4,128)} %copy.14), calls=%async_computation.1 | async-start | bytes 65536 | tf_op jit(solution)/shard_map/all_to_all | solution.py:43
  60.8 492.0 %all-reduce.2.cloned.1.call-start = ((), (), s32[]{:S(2)}) async-start(), calls=%async_computation.2 | async-start | bytes 786432 | tf_op jit(solution)/shard_map/psum | solution.py:64
  67.2 1.1 copy-start.10
  69.1 1.0 copy-start.2
  69.1 1.0 copy-start.4
  70.1 1.1 copy-start.11
  71.2 1.1 copy-start.10
  73.1 1.0 copy-start.2
  73.1 1.0 copy-start.4
  74.1 1.1 copy-start.11
  75.2 1.1 copy-start.10
  77.1 1.0 copy-start.2
  77.1 1.0 copy-start.4
  78.1 1.1 copy-start.11
  79.3 1.1 copy-start.10
  81.1 1.0 copy-start.2
  81.1 1.0 copy-start.4
  82.1 1.1 copy-start.11
  85.6 2.4 copy-start.8
  85.6 2.4 copy-start.9
Sparse Core Ops, SparseCore 0:
  88.1 464.7 all-reduce.1
where the time goes:
time: 562 us; the launch traced here: 561 us
  waiting for transfers between devices  476 us (85%)
  blocking collectives  26.8 us (5%)
  matrix products  14.4 us (3%)
  between operations  14.2 us (3%)
  local copies, waits for them, and re-layouts  10.5 us (2%)
  starting transfers between devices  10.2 us (2%)
  other arithmetic  8.8 us (2%)
    psum x1, waiting for transfers between devices, body(): full_grad = lax.psum(partial_grad, ('query', 'passage'))  464 us
    all_gather x1, blocking collectives, body(): gathered = lax.all_gather(queries, 'passage', axis=0, tiled=True)  26.8 us
  transfers between devices with their start and end apart: 3, of which 3 were waited for; matrix products, arithmetic and copies ran while one was open for 0% of the time, Pallas kernels for 0%

commit v1 on v0

--- a/solution.py
+++ b/solution.py
@@ -18,7 +18,14 @@
     norm = jnp.sqrt(jnp.sum(flat * flat, axis=1, keepdims=True) + EPS)
     unit = flat / norm
     embed = unit.astype(jnp.bfloat16).reshape(pcount, ptok, width)
-    gathered = lax.all_gather(queries, "passage", axis=0, tiled=True)
+    ring = [queries]
+    for hop in range(15):
+        ring.append(lax.ppermute(ring[-1], "passage", [(dev, (dev + 1) % 16) for dev in range(16)]))
+    gathered = jnp.roll(
+        jnp.concatenate(ring[::-1], axis=0),
+        (lax.axis_index("passage") + 1) * ring[0].shape[0],
+        axis=0,
+    )
     qflat = gathered.reshape(-1, width)
 
     def score_single(emb):

time: 562 us -> 657 us (1.17)
  waiting for transfers between devices: 476 us -> 567 us
  starting transfers between devices: 10.2 us -> 55.7 us
  blocking collectives: 26.8 us -> 0 us
    ppermute x0 -> x15, waiting for transfers between devices: none -> 92.8 us  [body(): lax.ppermute(ring[-1], 'passage', [(dev, (dev + 1) % 16) for dev in range...]
    ppermute x0 -> x15, starting transfers between devices: none -> 30.3 us  [body(): lax.ppermute(ring[-1], 'passage', [(dev, (dev + 1) % 16) for dev in range...]
    all_gather x1 -> x0, blocking collectives: 26.8 us -> none  [body(): gathered = lax.all_gather(queries, 'passage', axis=0, tiled=True)]
    all_to_all x1, starting transfers between devices: 5.41 us -> 20.6 us  [body(): lax.all_to_all(scores, 'passage', split_axis=0, concat_axis=1, tiled=True)]
  transfers between devices with their start and end apart: 3 -> 18, of which waited for: 3 -> 18; matrix products, arithmetic and copies ran while one was open for 0% -> 0% of each run, Pallas kernels for 0% -> 0%
where the time goes in v1:
time: 657 us; the launch traced here: 656 us
  waiting for transfers between devices  567 us (86%)
  starting transfers between devices  55.7 us (8%)
  between operations  14.5 us (2%)
  matrix products  8.42 us (1%)
  local copies, waits for them, and re-layouts  6.82 us (1%)
    psum x1, waiting for transfers between devices, body(): full_grad = lax.psum(partial_grad, ('query', 'passage'))  462 us
    ppermute x15, waiting for transfers between devices, body(): lax.ppermute(ring[-1], 'passage', [(dev, (dev + 1) % 16) for dev in range...  92.8 us
    ppermute x15, starting transfers between devices, body(): lax.ppermute(ring[-1], 'passage', [(dev, (dev + 1) % 16) for dev in range...  30.3 us
    all_to_all x1, starting transfers between devices, body(): lax.all_to_all(scores, 'passage', split_axis=0, concat_axis=1, tiled=True)  20.6 us
  transfers between devices with their start and end apart: 18, of which 18 were waited for; matrix products, arithmetic and copies ran while one was open for 0% of the time, Pallas kernels for 0%

profile of v1, /device:TPU:2, one launch (start us, length us, event | category | flops | bytes accessed | tf_op | source)
XLA Modules:
  0.0 656.2 jit_solution(12542240478238692443)
XLA Ops:
  7.2 3.6 collective-permute-start
  10.8 4.6 collective-permute-done
  15.4 1.9 collective-permute-start.1
  17.4 6.0 collective-permute-done.1
  23.3 1.9 collective-permute-start.2
  25.3 6.0 collective-permute-done.2
  31.3 1.9 collective-permute-start.3
  33.2 6.0 collective-permute-done.3
  39.2 1.9 collective-permute-start.4
  41.1 6.0 collective-permute-done.4
  47.1 1.9 collective-permute-start.5
  49.0 6.2 collective-permute-done.5
  55.2 1.9 collective-permute-start.6
  57.1 6.0 collective-permute-done.6
  63.1 1.9 collective-permute-start.7
  65.0 6.0 collective-permute-done.7
  71.0 1.9 collective-permute-start.8
  72.9 6.0 collective-permute-done.8
  78.9 1.9 collective-permute-start.9
  80.8 6.5 collective-permute-done.9
  87.4 1.9 collective-permute-start.10
  89.3 7.5 %collective-permute-done.10 = bf16[4,32,128]{2,1,0:T(8,128)(2,1)S(1)} collective-permute-done((bf16[4,32,128]{2,1,0:T(8,128)(2,1)S(1)}, bf16[4,32,128]{2,1,0:T(8,128)(2,1)S(1)}, u32[]{:S(2)}, u32[]{:S(2)}) %collective-permute-start.10) | collective-permute-done | bytes 32800 | tf_op jit(solution)/shard_map/ppermute | solution.py:23
  96.8 1.9 collective-permute-start.11
  98.7 1.4 copy.11
  100.3 5.4 collective-permute-done.11
  105.8 1.9 collective-permute-start.12
  107.7 0.6 multiply_reduce_fusion.1
  108.2 6.5 collective-permute-done.12
  114.7 1.9 collective-permute-start.13
  116.7 7.2 %collective-permute-done.13 = bf16[4,32,128]{2,1,0:T(8,128)(2,1)S(1)} collective-permute-done((bf16[4,32,128]{2,1,0:T(8,128)(2,1)S(1)}, bf16[4,32,128]{2,1,0:T(8,128)(2,1)S(1)}, u32[]{:S(2)}, u32[]{:S(2)}) %collective-permute-start.13) | collective-permute-done | bytes 32800 | tf_op jit(solution)/shard_map/ppermute | solution.py:23
  123.8 1.9 collective-permute-start.14
  126.0 6.9 %collective-permute-done.14 = bf16[4,32,128]{2,1,0:T(8,128)(2,1)S(1)} collective-permute-done((bf16[4,32,128]{2,1,0:T(8,128)(2,1)S(1)}, bf16[4,32,128]{2,1,0:T(8,128)(2,1)S(1)}, u32[]{:S(2)}, u32[]{:S(2)}) %collective-permute-start.14) | collective-permute-done | bytes 32800 | tf_op jit(solution)/shard_map/ppermute | solution.py:23
  133.5 4.4 while.20
  138.0 0.6 copy.12
  138.6 20.6 %all-to-all-start = ((f32[16,4,4]{1,2,0:T(4,128)}), f32[16,4,4]{1,2,0:T(4,128)S(1)}, u32[]{:S(2)}, u32[]{:S(2)}) async-start(f32[16,4,4]{1,2,0:T(4,128)} %copy.12), calls=%async_computation | async-start | bytes 65536 | tf_op jit(solution)/shard_map/all_to_all | solution.py:39
  159.2 6.3 all-to-all-done
  166.5 0.6 copy.14
  167.1 4.8 all-to-all-start.1
  172.0 6.2 all-to-all-done.1
  178.3 5.6 while.21
  178.4 0.5 fusion.44
  179.8 0.5 fusion.44
  182.6 0.5 fusion.44
  184.2 1.3 convolution_bitcast_fusion.1
  185.6 0.5 fusion.18
  186.1 461.5 %all-reduce.2.cloned.1.call-done = f32[768,128]{0,1:T(8,128)} async-done(((f32[768,128]{0,1:T(8,128)}), f32[768,128]{0,1:T(8,128)}) %all-reduce.2.cloned.1.call-update) | async-done | bytes 393232 | tf_op jit(solution)/shard_map/psum | solution.py:71
  647.6 1.0 constant_dynamic-slice_fusion.1
  648.6 0.7 copy.16
  (120 shorter events, 10.6 us)
Async XLA Ops:
  7.2 100.5 %copy-start = (bf16[768,128]{1,0:T(8,128)(2,1)S(1)}, bf16[768,128]{1,0:T(8,128)(2,1)}, u32[]{:S(2)}) copy-start(bf16[768,128]{1,0:T(8,128)(2,1)} %param.10) | copy-start | bytes 589828
  7.2 8.3 %collective-permute-start = (bf16[4,32,128]{2,1,0:T(8,128)(2,1)}, bf16[4,32,128]{2,1,0:T(8,128)(2,1)S(1)}, u32[]{:S(2)}, u32[]{:S(2)}) collective-permute-start(bf16[4,32,128]{2,1,0:T(8,128)(2,1)} %param.8), channel_id=1, source_target_pairs={{0,1},{1,2},{2,3},{3,4},{4,5},{5,6},{6,7},{7,8},{8,9},{9,10},{10,1... | collective-permute-start | bytes 98312 | tf_op jit(solution)/shard_map/ppermute | solution.py:23
  15.4 7.9 %collective-permute-start.1 = (bf16[4,32,128]{2,1,0:T(8,128)(2,1)S(1)}, bf16[4,32,128]{2,1,0:T(8,128)(2,1)S(1)}, u32[]{:S(2)}, u32[]{:S(2)}) collective-permute-start(bf16[4,32,128]{2,1,0:T(8,128)(2,1)S(1)} %collective-permute-done), channel_id=1, source_target_pairs={{0,1},{1,2},{2,3},{3,4},{4,5},{5,6},{6,7},{7,8},{8,9},{9,10},{10,1... | collective-permute-start | bytes 98312 | tf_op jit(solution)/shard_map/ppermute | solution.py:23
  23.3 7.9 %collective-permute-start.2 = (bf16[4,32,128]{2,1,0:T(8,128)(2,1)S(1)}, bf16[4,32,128]{2,1,0:T(8,128)(2,1)S(1)}, u32[]{:S(2)}, u32[]{:S(2)}) collective-permute-start(bf16[4,32,128]{2,1,0:T(8,128)(2,1)S(1)} %collective-permute-done.1), channel_id=1, source_target_pairs={{0,1},{1,2},{2,3},{3,4},{4,5},{5,6},{6,7},{7,8},{8,9},{9,10},{10,1... | collective-permute-start | bytes 98312 | tf_op jit(solution)/shard_map/ppermute | solution.py:23
  31.3 7.9 %collective-permute-start.3 = (bf16[4,32,128]{2,1,0:T(8,128)(2,1)S(1)}, bf16[4,32,128]{2,1,0:T(8,128)(2,1)S(1)}, u32[]{:S(2)}, u32[]{:S(2)}) collective-permute-start(bf16[4,32,128]{2,1,0:T(8,128)(2,1)S(1)} %collective-permute-done.2), channel_id=1, source_target_pairs={{0,1},{1,2},{2,3},{3,4},{4,5},{5,6},{6,7},{7,8},{8,9},{9,10},{10,1... | collective-permute-start | bytes 98312 | tf_op jit(solution)/shard_map/ppermute | solution.py:23
  39.2 7.9 %collective-permute-start.4 = (bf16[4,32,128]{2,1,0:T(8,128)(2,1)S(1)}, bf16[4,32,128]{2,1,0:T(8,128)(2,1)S(1)}, u32[]{:S(2)}, u32[]{:S(2)}) collective-permute-start(bf16[4,32,128]{2,1,0:T(8,128)(2,1)S(1)} %collective-permute-done.3), channel_id=1, source_target_pairs={{0,1},{1,2},{2,3},{3,4},{4,5},{5,6},{6,7},{7,8},{8,9},{9,10},{10,1... | collective-permute-start | bytes 98312 | tf_op jit(solution)/shard_map/ppermute | solution.py:23
  47.1 8.1 %collective-permute-start.5 = (bf16[4,32,128]{2,1,0:T(8,128)(2,1)S(1)}, bf16[4,32,128]{2,1,0:T(8,128)(2,1)S(1)}, u32[]{:S(2)}, u32[]{:S(2)}) collective-permute-start(bf16[4,32,128]{2,1,0:T(8,128)(2,1)S(1)} %collective-permute-done.4), channel_id=1, source_target_pairs={{0,1},{1,2},{2,3},{3,4},{4,5},{5,6},{6,7},{7,8},{8,9},{9,10},{10,1... | collective-permute-start | bytes 98312 | tf_op jit(solution)/shard_map/ppermute | solution.py:23
  55.2 7.9 %collective-permute-start.6 = (bf16[4,32,128]{2,1,0:T(8,128)(2,1)S(1)}, bf16[4,32,128]{2,1,0:T(8,128)(2,1)S(1)}, u32[]{:S(2)}, u32[]{:S(2)}) collective-permute-start(bf16[4,32,128]{2,1,0:T(8,128)(2,1)S(1)} %collective-permute-done.5), channel_id=1, source_target_pairs={{0,1},{1,2},{2,3},{3,4},{4,5},{5,6},{6,7},{7,8},{8,9},{9,10},{10,1... | collective-permute-start | bytes 98312 | tf_op jit(solution)/shard_map/ppermute | solution.py:23
  63.1 7.9 %collective-permute-start.7 = (bf16[4,32,128]{2,1,0:T(8,128)(2,1)S(1)}, bf16[4,32,128]{2,1,0:T(8,128)(2,1)S(1)}, u32[]{:S(2)}, u32[]{:S(2)}) collective-permute-start(bf16[4,32,128]{2,1,0:T(8,128)(2,1)S(1)} %collective-permute-done.6), channel_id=1, source_target_pairs={{0,1},{1,2},{2,3},{3,4},{4,5},{5,6},{6,7},{7,8},{8,9},{9,10},{10,1... | collective-permute-start | bytes 98312 | tf_op jit(solution)/shard_map/ppermute | solution.py:23
  71.0 7.9 %collective-permute-start.8 = (bf16[4,32,128]{2,1,0:T(8,128)(2,1)S(1)}, bf16[4,32,128]{2,1,0:T(8,128)(2,1)S(1)}, u32[]{:S(2)}, u32[]{:S(2)}) collective-permute-start(bf16[4,32,128]{2,1,0:T(8,128)(2,1)S(1)} %collective-permute-done.7), channel_id=1, source_target_pairs={{0,1},{1,2},{2,3},{3,4},{4,5},{5,6},{6,7},{7,8},{8,9},{9,10},{10,1... | collective-permute-start | bytes 98312 | tf_op jit(solution)/shard_map/ppermute | solution.py:23
  78.9 8.5 %collective-permute-start.9 = (bf16[4,32,128]{2,1,0:T(8,128)(2,1)S(1)}, bf16[4,32,128]{2,1,0:T(8,128)(2,1)S(1)}, u32[]{:S(2)}, u32[]{:S(2)}) collective-permute-start(bf16[4,32,128]{2,1,0:T(8,128)(2,1)S(1)} %collective-permute-done.8), channel_id=1, source_target_pairs={{0,1},{1,2},{2,3},{3,4},{4,5},{5,6},{6,7},{7,8},{8,9},{9,10},{10,1... | collective-permute-start | bytes 98312 | tf_op jit(solution)/shard_map/ppermute | solution.py:23
  87.4 9.4 %collective-permute-start.10 = (bf16[4,32,128]{2,1,0:T(8,128)(2,1)S(1)}, bf16[4,32,128]{2,1,0:T(8,128)(2,1)S(1)}, u32[]{:S(2)}, u32[]{:S(2)}) collective-permute-start(bf16[4,32,128]{2,1,0:T(8,128)(2,1)S(1)} %collective-permute-done.9), channel_id=1, source_target_pairs={{0,1},{1,2},{2,3},{3,4},{4,5},{5,6},{6,7},{7,8},{8,9},{9,10},{10,1... | collective-permute-start | bytes 98312 | tf_op jit(solution)/shard_map/ppermute | solution.py:23
  96.8 9.0 %collective-permute-start.11 = (bf16[4,32,128]{2,1,0:T(8,128)(2,1)S(1)}, bf16[4,32,128]{2,1,0:T(8,128)(2,1)S(1)}, u32[]{:S(2)}, u32[]{:S(2)}) collective-permute-start(bf16[4,32,128]{2,1,0:T(8,128)(2,1)S(1)} %collective-permute-done.10), channel_id=1, source_target_pairs={{0,1},{1,2},{2,3},{3,4},{4,5},{5,6},{6,7},{7,8},{8,9},{9,10},{10,1... | collective-permute-start | bytes 98312 | tf_op jit(solution)/shard_map/ppermute | solution.py:23
  100.3 32.9 %copy-start.1 = (bf16[4,32,128]{2,1,0:T(8,128)(2,1)S(1)}, bf16[4,32,128]{2,1,0:T(8,128)(2,1)}, u32[]{:S(2)}) copy-start(bf16[4,32,128]{2,1,0:T(8,128)(2,1)} %param.8) | copy-start | bytes 98308
  105.8 9.0 %collective-permute-start.12 = (bf16[4,32,128]{2,1,0:T(8,128)(2,1)S(1)}, bf16[4,32,128]{2,1,0:T(8,128)(2,1)S(1)}, u32[]{:S(2)}, u32[]{:S(2)}) collective-permute-start(bf16[4,32,128]{2,1,0:T(8,128)(2,1)S(1)} %collective-permute-done.11), channel_id=1, source_target_pairs={{0,1},{1,2},{2,3},{3,4},{4,5},{5,6},{6,7},{7,8},{8,9},{9,10},{10,1... | collective-permute-start | bytes 98312 | tf_op jit(solution)/shard_map/ppermute | solution.py:23
  114.7 9.1 %collective-permute-start.13 = (bf16[4,32,128]{2,1,0:T(8,128)(2,1)S(1)}, bf16[4,32,128]{2,1,0:T(8,128)(2,1)S(1)}, u32[]{:S(2)}, u32[]{:S(2)}) collective-permute-start(bf16[4,32,128]{2,1,0:T(8,128)(2,1)S(1)} %collective-permute-done.12), channel_id=1, source_target_pairs={{0,1},{1,2},{2,3},{3,4},{4,5},{5,6},{6,7},{7,8},{8,9},{9,10},{10,1... | collective-permute-start | bytes 98312 | tf_op jit(solution)/shard_map/ppermute | solution.py:23
  123.8 9.1 %collective-permute-start.14 = (bf16[4,32,128]{2,1,0:T(8,128)(2,1)S(1)}, bf16[4,32,128]{2,1,0:T(8,128)(2,1)S(1)}, u32[]{:S(2)}, u32[]{:S(2)}) collective-permute-start(bf16[4,32,128]{2,1,0:T(8,128)(2,1)S(1)} %collective-permute-done.13), channel_id=1, source_target_pairs={{0,1},{1,2},{2,3},{3,4},{4,5},{5,6},{6,7},{7,8},{8,9},{9,10},{10,1... | collective-permute-start | bytes 98312 | tf_op jit(solution)/shard_map/ppermute | solution.py:23
  133.5 32.0 %copy-start.2 = (s32[4,64]{1,0:T(4,128)S(1)}, s32[4,64]{1,0:T(4,128)}, u32[]{:S(2)}) copy-start(s32[4,64]{1,0:T(4,128)} %param.11) | copy-start | bytes 3076
  138.6 26.9 %all-to-all-start = ((f32[16,4,4]{1,2,0:T(4,128)}), f32[16,4,4]{1,2,0:T(4,128)S(1)}, u32[]{:S(2)}, u32[]{:S(2)}) async-start(f32[16,4,4]{1,2,0:T(4,128)} %copy.12), calls=%async_computation | async-start | bytes 65536 | tf_op jit(solution)/shard_map/all_to_all | solution.py:39
  167.1 11.1 %all-to-all-start.1 = ((f32[4,16,4]{2,0,1:T(4,128)}), f32[4,16,4]{2,0,1:T(4,128)S(1)}, u32[]{:S(2)}, u32[]{:S(2)}) async-start(f32[4,16,4]{2,0,1:T(4,128)} %copy.14), calls=%async_computation.1 | async-start | bytes 65536 | tf_op jit(solution)/shard_map/all_to_all | solution.py:50
  171.9 475.8 %all-reduce.2.cloned.1.call-start = ((), (), s32[]{:S(2)}) async-start(), calls=%async_computation.2 | async-start | bytes 786432 | tf_op jit(solution)/shard_map/psum | solution.py:71
Sparse Core Ops, SparseCore 0:
  185.7 461.8 all-reduce.1
